TPU v7x, 32 devices: a whole 2x2x4 slice. The times are simulated.
32 devices in a mesh: expert: 8 (over y, x, core), tensor: 4 (over z).
Axes of the slice: x: 2, y: 2, z: 4, core: 2. Of those that a mesh axis runs over, the one named last changes fastest.
Arguments:
- tokens: bfloat16 [2560, 4096], P('expert', 'tensor'), may hold values from -6 to 6
- grad_out: bfloat16 [2560, 4096], P('expert', 'tensor'), may hold values from -6 to 6
- routes: int32 [2560, 4], P('expert'), may hold values from 0 to 7, all different within a row; in each aligned block of 320 rows (0 to 319, 320 to 639, ...) at most 200 rows name the same one
- route_weights: float32 [2560, 4], P('expert'), may hold values from 0.05 to 0.5
- swap_flags: int32 [4], replicated, may hold values from 0 to 1023
- weights: bfloat16 [8, 3, 1536, 4096], P('expert', None, None, 'tensor'), may hold values from -0.09375 to 0.09375
- first_moment: bfloat16 [8, 3, 1536, 4096], P('expert', None, None, 'tensor'), may hold values from -8 to 8
- second_moment: bfloat16 [8, 3, 1536, 4096], P('expert', None, None, 'tensor'), may hold values from 1 to 30
Outputs:
- combined: bfloat16 [2560, 4096], P('expert', 'tensor')
- update: bfloat16 [8, 3, 1536, 4096], P('expert', None, None, 'tensor')
Inputs may be any that keep to these rules, and one draw needn't show every extreme that they name: `routes`: in each aligned block of 320 rows no expert is named by more than 200 rows, a bound that some block reaches; a row names 4 different experts.
All inputs are finite; a program needn't handle non-finite values.
Results may differ from a plain program's by a relative error of at most 0.023.
Values may be sent and summed in bfloat16 or wider, within the bound.
A program may use at most 192 MiB of HBM per device.

v0:
```python
import jax
import jax.numpy as jnp
from jax import lax
from jax.sharding import PartitionSpec as P

correction_one = 1.0 - 0.9**20
correction_two = 1.0 - 0.95**20


def from_partner(value, axis, distance):
    return lax.ppermute(value, axis, [(i, i ^ 1 << distance) for i in range(lax.axis_size(axis))])


def contract_last(left_rows, right_rows):
    return lax.dot_general(
        left_rows, right_rows, (((1,), (1,)), ((), ())), preferred_element_type=jnp.float32
    )


def contract_first(left_rows, right_rows):
    return lax.dot_general(
        left_rows, right_rows, (((0,), (0,)), ((), ())), preferred_element_type=jnp.float32
    )


def body(tokens, grad_out, routes, route_weights, swap_flags, weights, first_moment, second_moment):
    expert_count = lax.axis_size("expert")
    tok_count = routes.shape[0]
    route_count = routes.shape[1]
    feat_width = tokens.shape[1]
    slot_cap = tok_count * route_count * 5 // (4 * expert_count)
    slot_total = tok_count * route_count
    positions = jnp.arange(expert_count, dtype=jnp.int32)
    paired = jnp.repeat(jnp.bitwise_and(swap_flags, 1), 2)
    own_flag = jnp.sum(jnp.where(positions == lax.axis_index("expert"), paired, 0))
    moved = from_partner((weights, first_moment, second_moment), "expert", 0)
    traded = own_flag == 1
    weights = jnp.where(traded, moved[0], weights)
    first_moment = jnp.where(traded, moved[1], first_moment)
    second_moment = jnp.where(traded, moved[2], second_moment)
    destination = jnp.where(paired == 1, jnp.bitwise_xor(positions, 1), positions)
    flat_ids = routes.reshape(-1)
    id_onehot = (flat_ids[:, None] == positions[None, :]).astype(jnp.int32)
    dest_ids = jnp.sum(id_onehot * destination[None, :], axis=1)
    dest_onehot = (dest_ids[:, None] == positions[None, :]).astype(jnp.int32)
    slot_rank = jnp.sum((jnp.cumsum(dest_onehot, axis=0) - dest_onehot) * dest_onehot, axis=1)
    slot_index = dest_ids * slot_cap + slot_rank
    table_rows = (
        jnp.full((expert_count * slot_cap,), slot_total, jnp.int32)
        .at[slot_index]
        .set(jnp.arange(slot_total, dtype=jnp.int32))
    )
    token_pad = jnp.concatenate([tokens, jnp.zeros((1, feat_width), tokens.dtype)], axis=0)
    scaled_grad = (route_weights[:, :, None] * grad_out[:, None, :].astype(jnp.float32)).astype(
        jnp.bfloat16
    )
    grad_pad = jnp.concatenate(
        [scaled_grad.reshape(slot_total, feat_width), jnp.zeros((1, feat_width), jnp.bfloat16)],
        axis=0,
    )
    send_tokens = token_pad[table_rows // route_count].reshape(expert_count, slot_cap, feat_width)
    send_grads = grad_pad[table_rows].reshape(expert_count, slot_cap, feat_width)
    got_tokens, got_grads = (
        lax.all_to_all(send_tokens, "expert", split_axis=0, concat_axis=0, tiled=True),
        lax.all_to_all(send_grads, "expert", split_axis=0, concat_axis=0, tiled=True),
    )
    slot_rows = expert_count * slot_cap
    token_slots = got_tokens.reshape(slot_rows, feat_width)
    grad_slots = got_grads.reshape(slot_rows, feat_width)
    own_weights = weights[0]
    hidden_width = own_weights.shape[1]
    preact = lax.psum(
        contract_last(token_slots, own_weights[0:2].reshape(2 * hidden_width, feat_width)).astype(
            jnp.bfloat16
        ),
        "tensor",
    ).astype(jnp.float32)
    gate_pre = preact[:, :hidden_width]
    up_pre = preact[:, hidden_width:]
    sig_gate = jax.nn.sigmoid(gate_pre)
    hidden = (gate_pre * sig_gate * up_pre).astype(jnp.bfloat16)
    output_slots = jnp.dot(hidden, own_weights[2], preferred_element_type=jnp.float32).astype(
        jnp.bfloat16
    )
    returned = lax.all_to_all(
        output_slots.reshape(expert_count, slot_cap, feat_width),
        "expert",
        split_axis=0,
        concat_axis=0,
        tiled=True,
    )
    hidden_grad = lax.psum(
        contract_last(grad_slots, own_weights[2]).astype(jnp.bfloat16), "tensor"
    ).astype(jnp.float32)
    gate_grad = (hidden_grad * up_pre * sig_gate * (1.0 + gate_pre * (1.0 - sig_gate))).astype(
        jnp.bfloat16
    )
    up_grad = (hidden_grad * gate_pre * sig_gate).astype(jnp.bfloat16)
    weight_grad = jnp.stack(
        [
            contract_first(gate_grad, token_slots),
            contract_first(up_grad, token_slots),
            contract_first(hidden, grad_slots),
        ]
    )
    moment_new = 0.9 * first_moment[0].astype(jnp.float32) + 0.1 * weight_grad
    square_new = 0.95 * second_moment[0].astype(jnp.float32) + 0.05 * weight_grad * weight_grad
    step_dir = moment_new / correction_one / (jnp.sqrt(square_new / correction_two) + 1e-08)
    update = step_dir.astype(jnp.bfloat16)[None]
    back_slots = returned.reshape(slot_rows, feat_width)
    gathered_out = (
        back_slots[slot_index].reshape(tok_count, route_count, feat_width).astype(jnp.float32)
    )
    combined = jnp.sum(route_weights[:, :, None] * gathered_out, axis=1).astype(jnp.bfloat16)
    return (combined, update)


def solution(mesh):
    placed = (
        P("expert", "tensor"),
        P("expert", "tensor"),
        P("expert", None),
        P("expert", None),
        P(),
        P("expert", None, None, "tensor"),
        P("expert", None, None, "tensor"),
        P("expert", None, None, "tensor"),
    )
    return jax.shard_map(
        body,
        mesh=mesh,
        in_specs=placed,
        out_specs=(P("expert", "tensor"), P("expert", None, None, "tensor")),
        check_vma=False,
    )
```

profile of v0, /device:TPU:0, one launch (start us, length us, event | category | flops | bytes accessed | tf_op | source)
XLA Modules:
  0.0 758.2 jit_solution(17305862190993749333)
XLA Ops:
  7.2 0.6 collective-permute-start
  7.7 0.7 broadcast_compare_fusion
  8.4 0.1 broadcast_in_dim.15
  8.5 0.1 eq.64
  8.6 0.8 copy.15
  9.4 0.1 eq.59
  9.5 0.1 select_reduce_fusion
  9.6 2.3 reduce-window.6
  11.9 0.3 slice_reduce_fusion
  12.2 0.2 reduce-window.9
  12.4 4.9 mul.138
  17.2 7.3 mul.139
  24.5 0.1 copy.14
  24.7 0.1 mul.136
  24.8 0.5 copy-done.4
  25.3 2.8 multiply_convert_fusion.1
  28.2 0.2 concatenate.26
  28.4 0.1 add_bitcast_fusion
  28.6 5.2 scatter_custom_fusion
  33.9 6.4 gather_fusion.2
  40.3 4.8 all-to-all-start.2
  45.2 6.5 gather_fusion
  51.7 33.2 %all-to-all-done.2 = bf16[8,200,1024]{2,1,0:T(8,128)(2,1)} async-done(((bf16[8,200,1024]{2,1,0:T(8,128)(2,1)}), bf16[8,200,1024]{2,1,0:T(8,128)(2,1)}, u32[]{:S(2)}, u32[]{:S(2)}) %all-to-all-start.2) | async-done | bytes 3276832 | tf_op jit(solution)/shard_map/all_to_all | solution.py:65
  85.0 3.7 all-to-all-start
  88.6 0.2 all-reduce.5.cloned.1.call-start
  88.9 0.6 fusion.30
  90.2 5.4 broadcast_select_fusion
  95.6 3.8 slice.34
  99.4 1.8 copy-done
  101.2 9.0 %convolution_convert_fusion.1 = bf16[1600,1536]{1,0:T(8,128)(2,1)} fusion(bf16[1600,1024]{1,0:T(8,128)(2,1)} %bitcast.9, bf16[1,3,1536,1024]{3,2,1,0:T(8,128)(2,1)S(1)} %broadcast_select_fusion), kind=kOutput, calls=%fused_computation.23 | convolution fusion | flops 5035622400 | bytes 11337728 | tf_op jit(solution)/shard_map/dot_general | solution.py:15
  110.2 17.6 %all-to-all-done = bf16[8,200,1024]{2,1,0:T(8,128)(2,1)S(1)} async-done(((bf16[8,200,1024]{2,1,0:T(8,128)(2,1)}), bf16[8,200,1024]{2,1,0:T(8,128)(2,1)S(1)}, u32[]{:S(2)}, u32[]{:S(2)}) %all-to-all-start) | async-done | bytes 3276832 | tf_op jit(solution)/shard_map/all_to_all | solution.py:64
  127.8 16.5 %convolution_convert_fusion = bf16[1600,3072]{1,0:T(8,128)(2,1)} fusion(bf16[1600,1024]{1,0:T(8,128)(2,1)S(1)} %bitcast.51, bf16[3072,1024]{1,0:T(8,128)(2,1)} %bitcast.50), kind=kOutput, calls=%fused_computation.14 | convolution fusion | flops 10071244800 | bytes 19398656 | tf_op jit(solution)/shard_map/dot_general | solution.py:15
  144.3 0.0 all-reduce.5.cloned.1.call-update
  144.3 0.1 collective-permute-start.2
  144.4 0.5 collective-permute-start.1
  144.9 494.9 %all-reduce.5.cloned.1.call-done = (bf16[1600,3072]{1,0:T(8,128)(2,1)}, bf16[1600,1536]{1,0:T(8,128)(2,1)}) async-done(((bf16[1600,3072]{1,0:T(8,128)(2,1)}, bf16[1600,1536]{1,0:T(8,128)(2,1)}), (bf16[1600,3072]{1,0:T(8,128)(2,1)}, bf16[1600,1536]{1,0:T(8,128)(2,1)})) %all-reduce.5.cloned.1.call-update) | async-done | bytes 14745616 | tf_op jit(solution)/shard_map/psum | solution.py:72
  639.9 12.8 %convert_element_type.64 = f32[1600,3072]{1,0:T(8,128)} convert(bf16[1600,3072]{1,0:T(8,128)(2,1)} %get-tuple-element.2) | non-fusion elementwise | flops 4915200 | bytes 29491200 | tf_op jit(solution)/shard_map/convert_element_type | solution.py:77
  652.7 8.2 %multiply_convert_fusion = bf16[1600,1536]{1,0:T(8,128)(2,1)S(1)} fusion(f32[1600,3072]{1,0:T(8,128)} %convert_element_type.64), kind=kLoop, calls=%fused_computation.20 | loop fusion | flops 14745600 | bytes 24576000 | tf_op jit(solution)/shard_map/convert_element_type | solution.py:81
  660.9 10.3 %convolution_convert_fusion.2 = bf16[1600,1024]{1,0:T(8,128)(2,1)} fusion(bf16[1600,1536]{1,0:T(8,128)(2,1)S(1)} %multiply_convert_fusion, bf16[1,3,1536,1024]{3,2,1,0:T(8,128)(2,1)} %copy-done), kind=kOutput, calls=%fused_computation.31 | convolution fusion | flops 5034803200 | bytes 11337728 | tf_op jit(solution)/shard_map/dot_general | solution.py:82
  671.2 3.9 all-to-all-start.1
  675.1 9.1 %convolution_bitcast_fusion = f32[1,1,1536,1024]{3,2,1,0:T(8,128)S(1)} fusion(bf16[1600,1536]{1,0:T(8,128)(2,1)} %copy-done.1, bf16[1600,1024]{1,0:T(8,128)(2,1)} %bitcast.9), kind=kOutput, calls=%fused_computation.30 | convolution fusion | flops 5033164800 | bytes 14483456 | tf_op jit(solution)/shard_map/dot_general | solution.py:21
  684.2 0.0 slice-start
  684.2 11.4 %fusion.18 = f32[1,1,1536,1024]{3,2,1,0:T(8,128)} fusion(bf16[1600,1024]{1,0:T(8,128)(2,1)S(1)} %bitcast.53, bf16[1600,1536]{1,0:T(8,128)(2,1)} %get-tuple-element.3, f32[1600,3072]{1,0:T(8,128)} %convert_element_type.64), kind=kOutput, calls=%fused_computation.29 | convolution fusion | flops 5050368000 | bytes 24313856 | tf_op jit(solution)/shard_map/dot_general | solution.py:21
  695.6 16.4 %fusion.15 = f32[1,1,1536,1024]{3,2,1,0:T(8,128)} fusion(bf16[1600,1024]{1,0:T(8,128)(2,1)} %bitcast.52, bf16[1600,1536]{1,0:T(8,128)(2,1)} %get-tuple-element.3, f32[1600,3072]{1,0:T(8,128)} %convert_element_type.64), kind=kOutput, calls=%fused_computation.28 | convolution fusion | flops 5060198400 | bytes 34144256 | tf_op jit(solution)/shard_map/dot_general | solution.py:21
  712.1 21.6 %fusion.5 = bf16[1,3,1536,1024]{3,2,1,0:T(8,128)(2,1)} fusion(f32[1,1,1536,1024]{3,2,1,0:T(8,128)S(1)} %convolution_bitcast_fusion, f32[1,1,1536,1024]{3,2,1,0:T(8,128)} %fusion.18, f32[1,1,1536,1024]{3,2,1,0:T(8,128)} %fusion.15, bf16[1,3,1536,1024]{3,2,1,0:T(8,128)(2,1)} %collective-permute-done.2, bf16[1,3,1536,1024]{3,2,1,0:T(8,128)(2,1)S(1)} %bitcast.49, ...), kind=kLoop, calls=%fused_computation.11 | loop fusion | flops 84934656 | bytes 66060288 | tf_op jit(solution)/shard_map/convert_element_type | solution.py:109
  733.7 5.1 gather_fusion.1
  738.8 5.9 reshape.227
  744.6 6.7 multiply_reduce_fusion
  (37 shorter events, 0.2 us)
Async XLA Ops:
  7.2 17.4 %copy-start.7 = (f32[320,4]{0,1:T(4,128)S(1)}, f32[320,4]{0,1:T(4,128)}, u32[]{:S(2)}) copy-start(f32[320,4]{0,1:T(4,128)} %param.11) | copy-start | bytes 15364
  7.2 83.0 %collective-permute-start = (bf16[1,3,1536,1024]{3,2,1,0:T(8,128)(2,1)}, bf16[1,3,1536,1024]{3,2,1,0:T(8,128)(2,1)}, u32[]{:S(2)}, u32[]{:S(2)}) collective-permute-start(bf16[1,3,1536,1024]{3,2,1,0:T(8,128)(2,1)} %param.13), channel_id=1, source_target_pairs={{0,4},{4,0},{8,12},{12,8},{16,20},{20,16},{24,28},{28,24},{1,5},{5... | collective-permute-start | bytes 28311560 | tf_op jit(solution)/shard_map/ppermute | solution.py:11
  24.7 0.7 copy-start.4
  33.9 11.3 %copy-start.6 = (bf16[320,1024]{1,0:T(8,128)(2,1)S(1)}, bf16[320,1024]{1,0:T(8,128)(2,1)}, u32[]{:S(2)}) copy-start(bf16[320,1024]{1,0:T(8,128)(2,1)} %param.8) | copy-start | bytes 1966084
  40.3 44.6 %all-to-all-start.2 = ((bf16[8,200,1024]{2,1,0:T(8,128)(2,1)}), bf16[8,200,1024]{2,1,0:T(8,128)(2,1)}, u32[]{:S(2)}, u32[]{:S(2)}) async-start(bf16[8,200,1024]{2,1,0:T(8,128)(2,1)} %bitcast.47), calls=%async_computation.2 | async-start | bytes 6553600 | tf_op jit(solution)/shard_map/all_to_all | solution.py:65
  45.2 43.6 %copy-start.8 = (s32[4]{0:T(128)S(1)}, s32[4]{0:T(128)}, u32[]{:S(2)}) copy-start(s32[4]{0:T(128)} %param.12) | copy-start | bytes 52
  85.0 42.9 %all-to-all-start = ((bf16[8,200,1024]{2,1,0:T(8,128)(2,1)}), bf16[8,200,1024]{2,1,0:T(8,128)(2,1)S(1)}, u32[]{:S(2)}, u32[]{:S(2)}) async-start(bf16[8,200,1024]{2,1,0:T(8,128)(2,1)} %bitcast.46), calls=%async_computation | async-start | bytes 6553600 | tf_op jit(solution)/shard_map/all_to_all | solution.py:64
  88.6 551.2 %all-reduce.5.cloned.1.call-start = ((), (), s32[]{:S(2)}) async-start(), calls=%async_computation.3 | async-start | bytes 29491200 | tf_op jit(solution)/shard_map/psum | solution.py:72
  95.6 5.6 copy-start
  127.8 16.5 %copy-start.2 = (bf16[8,200,1024]{2,1,0:T(8,128)(2,1)}, bf16[8,200,1024]{2,1,0:T(8,128)(2,1)S(1)}, u32[]{:S(2)}) copy-start(bf16[8,200,1024]{2,1,0:T(8,128)(2,1)S(1)} %all-to-all-done) | copy-start | bytes 9830404
  144.3 567.7 %collective-permute-start.2 = (bf16[1,3,1536,1024]{3,2,1,0:T(8,128)(2,1)}, bf16[1,3,1536,1024]{3,2,1,0:T(8,128)(2,1)}, u32[]{:S(2)}, u32[]{:S(2)}) collective-permute-start(bf16[1,3,1536,1024]{3,2,1,0:T(8,128)(2,1)} %param.15), channel_id=1, source_target_pairs={{0,4},{4,0},{8,12},{12,8},{16,20},{20,16},{24,28},{28,24},{1,5},{5... | collective-permute-start | bytes 28311560 | tf_op jit(solution)/shard_map/ppermute | solution.py:11
  144.4 567.6 %collective-permute-start.1 = (bf16[1,3,1536,1024]{3,2,1,0:T(8,128)(2,1)}, bf16[1,3,1536,1024]{3,2,1,0:T(8,128)(2,1)}, u32[]{:S(2)}, u32[]{:S(2)}) collective-permute-start(bf16[1,3,1536,1024]{3,2,1,0:T(8,128)(2,1)} %param.14), channel_id=1, source_target_pairs={{0,4},{4,0},{8,12},{12,8},{16,20},{20,16},{24,28},{28,24},{1,5},{5... | collective-permute-start | bytes 28311560 | tf_op jit(solution)/shard_map/ppermute | solution.py:11
  660.8 10.3 %copy-start.1 = (bf16[1600,1536]{1,0:T(8,128)(2,1)}, bf16[1600,1536]{1,0:T(8,128)(2,1)S(1)}, u32[]{:S(2)}) copy-start(bf16[1600,1536]{1,0:T(8,128)(2,1)S(1)} %multiply_convert_fusion) | copy-start | bytes 14745604
  671.2 62.5 %all-to-all-start.1 = ((bf16[8,200,1024]{2,1,0:T(8,128)(2,1)}), bf16[8,200,1024]{2,1,0:T(8,128)(2,1)S(1)}, u32[]{:S(2)}, u32[]{:S(2)}) async-start(bf16[8,200,1024]{2,1,0:T(8,128)(2,1)} %bitcast.54), calls=%async_computation.1 | async-start | bytes 6553600 | tf_op jit(solution)/shard_map/all_to_all | solution.py:85
  675.1 9.1 %copy-start.3 = (bf16[8,200,1024]{2,1,0:T(8,128)(2,1)S(1)}, bf16[8,200,1024]{2,1,0:T(8,128)(2,1)}, u32[]{:S(2)}) copy-start(bf16[8,200,1024]{2,1,0:T(8,128)(2,1)} %copy-done.2) | copy-start | bytes 9830404
  684.2 27.8 %slice-start = ((s8[9437184]{0:T(1024)(128)(4,1)}), s8[4194304]{0:T(1024)(128)(4,1)S(1)}, s32[]{:S(2)}) async-start(s8[9437184]{0:T(1024)(128)(4,1)} %bitcast.48), calls=%async_computation.4 | async-start | bytes 8388608
  684.2 27.8 %slice-start.1 = ((s8[9437184]{0:T(1024)(128)(4,1)}), s8[4194304]{0:T(1024)(128)(4,1)S(1)}, s32[]{:S(2)}) async-start(s8[9437184]{0:T(1024)(128)(4,1)} %bitcast.48), calls=%async_computation.5 | async-start | bytes 8388608
  695.6 16.4 %slice-start.2 = ((s8[9437184]{0:T(1024)(128)(4,1)}), s8[1048576]{0:T(1024)(128)(4,1)S(1)}, s32[]{:S(2)}) async-start(s8[9437184]{0:T(1024)(128)(4,1)} %bitcast.48), calls=%async_computation.6 | async-start | bytes 2097152
  733.7 10.9 %copy-start.5 = (f32[320,4]{1,0:T(8,128)S(1)}, f32[320,4]{1,0:T(8,128)}, u32[]{:S(2)}) copy-start(f32[320,4]{1,0:T(8,128)} %copy-done.4) | copy-start | bytes 15364
Sparse Core Ops, SparseCore 0:
  144.5 495.3 all-reduce.4
where the time goes:
time: 759 us; the launch traced here: 758 us
  waiting for transfers between devices  546 us (72%)
  matrix products  72.7 us (10%)
  other arithmetic  61.6 us (8%)
  local copies, waits for them, and re-layouts  49.4 us (7%)
  between operations  15 us (2%)
  starting transfers between devices  13.7 us (2%)
    psum x1, waiting for transfers between devices, body(): lax.psum(contract_last(token_slots, own_weights[0:2].reshape(2 * hidden_w...  495 us
    dot_general x3, matrix products, contract_first(): lax.dot_general(left_rows, right_rows, (((0,), (0,)), ((), ())), preferre...  36.9 us
    all_to_all x1, waiting for transfers between devices, body(): lax.all_to_all(send_grads, 'expert', split_axis=0, concat_axis=0, tiled=T...  33.2 us
    dot_general x2, matrix products, contract_last(): lax.dot_general(left_rows, right_rows, (((1,), (1,)), ((), ())), preferre...  25.5 us
    convert_element_type x1, other arithmetic, body(): update = step_dir.astype(jnp.bfloat16)[None]  21.6 us
    all_to_all x1, waiting for transfers between devices, body(): lax.all_to_all(send_tokens, 'expert', split_axis=0, concat_axis=0, tiled=...  17.6 us
  transfers between devices with their start and end apart: 7, of which 3 were waited for; matrix products, arithmetic and copies ran while one was open for 19% of the time, Pallas kernels for 0%

commit v1 on v0

--- a/solution.py
+++ b/solution.py
@@ -69,11 +69,14 @@
     grad_slots = got_grads.reshape(slot_rows, feat_width)
     own_weights = weights[0]
     hidden_width = own_weights.shape[1]
-    preact = lax.psum(
-        contract_last(token_slots, own_weights[0:2].reshape(2 * hidden_width, feat_width)).astype(
-            jnp.bfloat16
+    preact = jnp.sum(
+        lax.all_gather(
+            contract_last(
+                token_slots, own_weights[0:2].reshape(2 * hidden_width, feat_width)
+            ).astype(jnp.bfloat16),
+            "tensor",
         ),
-        "tensor",
+        axis=0,
     ).astype(jnp.float32)
     gate_pre = preact[:, :hidden_width]
     up_pre = preact[:, hidden_width:]

time: 759 us -> 1010 us (1.33); the launches traced: 758 us -> 997 us
  waiting for transfers between devices: 546 us -> 718 us
  blocking collectives: 0 us -> 43.3 us
  other arithmetic: 61.6 us -> 82.7 us
    all_gather x0 -> x1, waiting for transfers between devices: none -> 578 us  [body(): lax.all_gather(contract_last(token_slots, own_weights[0:2].reshape(2 * hi...]
    psum x1, waiting for transfers between devices: 495 us -> 114 us  [body(): lax.psum(contract_last(grad_slots, own_weights[2]).astype(jnp.bfloat16),...]
    all_to_all x0 -> x1, blocking collectives: none -> 43.3 us  [body(): lax.all_to_all(send_grads, 'expert', split_axis=0, concat_axis=0, tiled=T...]
    all_to_all x1 -> x0, waiting for transfers between devices: 33.2 us -> none  [body(): lax.all_to_all(send_grads, 'expert', split_axis=0, concat_axis=0, tiled=T...]
    reduce_sum x0 -> x1, other arithmetic: none -> 19.7 us  [body(): jnp.sum(lax.all_gather(contract_last(token_slots, own_weights[0:2].reshap...]
  transfers between devices with their start and end apart: 7 -> 7, of which waited for: 3 -> 3; matrix products, arithmetic and copies ran while one was open for 19% -> 17% of each run, Pallas kernels for 0% -> 0%
where the time goes in v1:
time: 1010 us; the launch traced here: 997 us
  waiting for transfers between devices  718 us (71%)
  other arithmetic  82.7 us (8%)
  matrix products  74.9 us (7%)
  local copies, waits for them, and re-layouts  53.4 us (5%)
  blocking collectives  43.3 us (4%)
  between operations  15.2 us (2%)
    all_gather x1, waiting for transfers between devices, body(): lax.all_gather(contract_last(token_slots, own_weights[0:2].reshape(2 * hi...  578 us
    psum x1, waiting for transfers between devices, body(): lax.psum(contract_last(grad_slots, own_weights[2]).astype(jnp.bfloat16),...  114 us
    all_to_all x1, blocking collectives, body(): lax.all_to_all(send_grads, 'expert', split_axis=0, concat_axis=0, tiled=T...  43.3 us
    dot_general x3, matrix products, contract_first(): lax.dot_general(left_rows, right_rows, (((0,), (0,)), ((), ())), preferre...  39.2 us
    all_to_all x1, waiting for transfers between devices, body(): lax.all_to_all(send_tokens, 'expert', split_axis=0, concat_axis=0, tiled=...  25.4 us
    dot_general x2, matrix products, contract_last(): lax.dot_general(left_rows, right_rows, (((1,), (1,)), ((), ())), preferre...  25.4 us
    convert_element_type x1, other arithmetic, body(): update = step_dir.astype(jnp.bfloat16)[None]  21.6 us
  transfers between devices with their start and end apart: 7, of which 3 were waited for; matrix products, arithmetic and copies ran while one was open for 17% of the time, Pallas kernels for 0%

profile of v1, /device:TPU:0, one launch (start us, length us, event | category | flops | bytes accessed | tf_op | source)
XLA Modules:
  0.0 997.0 jit_solution(1538970550415856058)
XLA Ops:
  7.2 0.6 collective-permute-start
  7.7 0.8 copy.15
  8.6 0.1 eq.59
  8.7 0.7 broadcast_compare_fusion
  9.4 0.1 broadcast_in_dim.15
  9.4 0.1 eq.64
  9.5 0.1 select_reduce_fusion
  9.6 2.3 reduce-window.6
  11.9 0.3 slice_reduce_fusion
  12.2 0.2 reduce-window.9
  12.4 1.1 concatenate.25
  13.5 0.1 add_bitcast_fusion
  13.7 5.2 scatter_custom_fusion
  19.0 6.4 gather_fusion
  25.4 4.8 all-to-all-start
  30.3 0.6 fusion.30
  31.6 5.4 broadcast_select_fusion
  37.1 3.7 copy-done
  40.8 3.4 slice.34
  44.2 25.4 %all-to-all-done = bf16[8,200,1024]{2,1,0:T(8,128)(2,1)S(1)} async-done(((bf16[8,200,1024]{2,1,0:T(8,128)(2,1)}), bf16[8,200,1024]{2,1,0:T(8,128)(2,1)S(1)}, u32[]{:S(2)}, u32[]{:S(2)}) %all-to-all-start) | async-done | bytes 3276832 | tf_op jit(solution)/shard_map/all_to_all | solution.py:64
  69.5 16.5 %convolution_convert_fusion = bf16[1600,3072]{1,0:T(8,128)(2,1)} fusion(bf16[1600,1024]{1,0:T(8,128)(2,1)S(1)} %bitcast.55, bf16[3072,1024]{1,0:T(8,128)(2,1)} %bitcast.54), kind=kOutput, calls=%fused_computation.14 | convolution fusion | flops 10071244800 | bytes 19398656 | tf_op jit(solution)/shard_map/dot_general | solution.py:15
  86.1 0.6 copy-done.7
  86.7 0.1 copy.14
  86.9 0.1 mul.136
  87.0 0.1 copy-done.6
  87.1 3.8 mul.138
  90.9 7.9 mul.139
  98.8 4.3 multiply_convert_fusion.1
  103.1 0.2 concatenate.26
  103.4 6.4 gather_fusion.2
  109.8 43.3 %all_to_all.15 = bf16[8,200,1024]{2,1,0:T(8,128)(2,1)S(1)} all-to-all(bf16[8,200,1024]{2,1,0:T(8,128)(2,1)} %bitcast.49), channel_id=1, replica_groups=mesh['expert'=8,'tensor'=4] {'expert'}, dimensions={0} | all-to-all | bytes 6553600 | tf_op jit(solution)/shard_map/all_to_all | solution.py:65
  153.1 1.7 copy-done.3
  154.8 8.8 convolution_convert_fusion.1
  163.8 0.5 collective-permute-start.2
  164.3 578.5 %all-gather.3.cloned.1.call-done = bf16[6400,3072]{1,0:T(8,128)(2,1)} async-done(((bf16[1600,3072]{1,0:T(8,128)(2,1)}), bf16[6400,3072]{1,0:T(8,128)(2,1)}) %all-gather.3.cloned.1.call-update) | async-done | bytes 39321616 | tf_op jit(solution)/shard_map/all_gather | solution.py:73
  742.8 19.7 %reduce_sum.51 = bf16[1600,3072]{1,0:T(8,128)(2,1)} reduce(bf16[4,1600,3072]{2,1,0:T(8,128)(2,1)} %bitcast.47, bf16[]{:T(256)} %constant.22.clone.1), dimensions={0}, to_apply=%region_6.7 | reduce | flops 14745600 | bytes 49152000 | tf_op jit(solution)/shard_map/reduce_sum | solution.py:72
  762.5 12.8 %convert_element_type.66 = f32[1600,3072]{1,0:T(8,128)} convert(bf16[1600,3072]{1,0:T(8,128)(2,1)} %reduce_sum.51) | non-fusion elementwise | flops 4915200 | bytes 29491200 | tf_op jit(solution)/shard_map/convert_element_type | solution.py:80
  775.3 8.2 multiply_convert_fusion
  783.5 10.3 %convolution_convert_fusion.2 = bf16[1600,1024]{1,0:T(8,128)(2,1)} fusion(bf16[1600,1536]{1,0:T(8,128)(2,1)S(1)} %multiply_convert_fusion, bf16[1,3,1536,1024]{3,2,1,0:T(8,128)(2,1)} %copy-done), kind=kOutput, calls=%fused_computation.31 | convolution fusion | flops 5034803200 | bytes 11337728 | tf_op jit(solution)/shard_map/dot_general | solution.py:85
  793.8 3.8 all-to-all-start.1
  797.7 10.5 %convolution_bitcast_fusion = f32[1,1,1536,1024]{3,2,1,0:T(8,128)} fusion(bf16[1600,1536]{1,0:T(8,128)(2,1)} %copy-done.1, bf16[1600,1024]{1,0:T(8,128)(2,1)} %bitcast.59), kind=kOutput, calls=%fused_computation.30 | convolution fusion | flops 5033164800 | bytes 14483456 | tf_op jit(solution)/shard_map/dot_general | solution.py:21
  808.1 113.7 %all-reduce.4.cloned.1.call-done = bf16[1600,1536]{1,0:T(8,128)(2,1)} async-done(((bf16[1600,1536]{1,0:T(8,128)(2,1)}), bf16[1600,1536]{1,0:T(8,128)(2,1)}) %all-reduce.4.cloned.1.call-update) | async-done | bytes 4915216 | tf_op jit(solution)/shard_map/psum | solution.py:95
  921.9 12.2 %fusion.18 = f32[1,1,1536,1024]{3,2,1,0:T(8,128)} fusion(bf16[1600,1024]{1,0:T(8,128)(2,1)} %bitcast.56, bf16[1600,1536]{1,0:T(8,128)(2,1)} %all-reduce.4.cloned.1.call-done, f32[1600,3072]{1,0:T(8,128)} %convert_element_type.66), kind=kOutput, calls=%fused_computation.29 | convolution fusion | flops 5050368000 | bytes 24313856 | tf_op jit(solution)/shard_map/dot_general | solution.py:21
  934.1 16.5 %fusion.15 = f32[1,1,1536,1024]{3,2,1,0:T(8,128)} fusion(bf16[1600,1024]{1,0:T(8,128)(2,1)} %bitcast.57, bf16[1600,1536]{1,0:T(8,128)(2,1)} %all-reduce.4.cloned.1.call-done, f32[1600,3072]{1,0:T(8,128)} %convert_element_type.66), kind=kOutput, calls=%fused_computation.28 | convolution fusion | flops 5060198400 | bytes 34144256 | tf_op jit(solution)/shard_map/dot_general | solution.py:21
  950.6 21.6 %fusion.5 = bf16[1,3,1536,1024]{3,2,1,0:T(8,128)(2,1)} fusion(f32[1,1,1536,1024]{3,2,1,0:T(8,128)S(1)} %bitcast.53, f32[1,1,1536,1024]{3,2,1,0:T(8,128)} %fusion.18, f32[1,1,1536,1024]{3,2,1,0:T(8,128)} %fusion.15, bf16[1,3,1536,1024]{3,2,1,0:T(8,128)(2,1)} %collective-permute-done.2, bf16[1,3,1536,1024]{3,2,1,0:T(8,128)(2,1)S(1)} %bitcast.51, ...), kind=kLoop, calls=%fused_computation.11 | loop fusion | flops 84934656 | bytes 66060288 | tf_op jit(solution)/shard_map/convert_element_type | solution.py:112
  972.2 5.1 gather_fusion.1
  977.3 5.9 reshape.227
  983.2 6.7 multiply_reduce_fusion
  (45 shorter events, 0.4 us)
Async XLA Ops:
  7.2 24.5 %collective-permute-start = (bf16[1,3,1536,1024]{3,2,1,0:T(8,128)(2,1)}, bf16[1,3,1536,1024]{3,2,1,0:T(8,128)(2,1)}, u32[]{:S(2)}, u32[]{:S(2)}) collective-permute-start(bf16[1,3,1536,1024]{3,2,1,0:T(8,128)(2,1)} %param.13), channel_id=1, source_target_pairs={{0,4},{4,0},{8,12},{12,8},{16,20},{20,16},{24,28},{28,24},{1,5},{5... | collective-permute-start | bytes 28311560 | tf_op jit(solution)/shard_map/ppermute | solution.py:11
  19.0 11.3 %copy-start.8 = (s32[4]{0:T(128)S(1)}, s32[4]{0:T(128)}, u32[]{:S(2)}) copy-start(s32[4]{0:T(128)} %param.12) | copy-start | bytes 52
  25.4 44.1 %all-to-all-start = ((bf16[8,200,1024]{2,1,0:T(8,128)(2,1)}), bf16[8,200,1024]{2,1,0:T(8,128)(2,1)S(1)}, u32[]{:S(2)}, u32[]{:S(2)}) async-start(bf16[8,200,1024]{2,1,0:T(8,128)(2,1)} %bitcast.48), calls=%async_computation | async-start | bytes 6553600 | tf_op jit(solution)/shard_map/all_to_all | solution.py:64
  30.3 712.5 %all-gather.3.cloned.1.call-start = ((), (), s32[]{:S(2)}) async-start(), calls=%async_computation.4 | async-start | bytes 49152000 | tf_op jit(solution)/shard_map/all_gather | solution.py:73
  37.1 3.7 copy-start
  69.5 16.5 %copy-start.2 = (bf16[8,200,1024]{2,1,0:T(8,128)(2,1)}, bf16[8,200,1024]{2,1,0:T(8,128)(2,1)S(1)}, u32[]{:S(2)}) copy-start(bf16[8,200,1024]{2,1,0:T(8,128)(2,1)S(1)} %all-to-all-done) | copy-start | bytes 9830404
  86.0 0.7 copy-start.7
  86.0 1.1 copy-start.6
  86.1 835.8 %all-reduce.4.cloned.1.call-start = ((), (), s32[]{:S(2)}) async-start(), calls=%async_computation.3 | async-start | bytes 9830400 | tf_op jit(solution)/shard_map/psum | solution.py:95
  86.9 11.9 %copy-start.4 = (f32[320,4]{1,0:T(8,128)}, f32[320,4]{1,0:T(8,128)S(1)}, u32[]{:S(2)}) copy-start(f32[320,4]{1,0:T(8,128)S(1)} %copy.14) | copy-start | bytes 15364
  153.1 1.7 copy-start.3
  163.7 786.9 %collective-permute-start.1 = (bf16[1,3,1536,1024]{3,2,1,0:T(8,128)(2,1)}, bf16[1,3,1536,1024]{3,2,1,0:T(8,128)(2,1)}, u32[]{:S(2)}, u32[]{:S(2)}) collective-permute-start(bf16[1,3,1536,1024]{3,2,1,0:T(8,128)(2,1)} %param.14), channel_id=1, source_target_pairs={{0,4},{4,0},{8,12},{12,8},{16,20},{20,16},{24,28},{28,24},{1,5},{5... | collective-permute-start | bytes 28311560 | tf_op jit(solution)/shard_map/ppermute | solution.py:11
  163.8 786.8 %collective-permute-start.2 = (bf16[1,3,1536,1024]{3,2,1,0:T(8,128)(2,1)}, bf16[1,3,1536,1024]{3,2,1,0:T(8,128)(2,1)}, u32[]{:S(2)}, u32[]{:S(2)}) collective-permute-start(bf16[1,3,1536,1024]{3,2,1,0:T(8,128)(2,1)} %param.15), channel_id=1, source_target_pairs={{0,4},{4,0},{8,12},{12,8},{16,20},{20,16},{24,28},{28,24},{1,5},{5... | collective-permute-start | bytes 28311560 | tf_op jit(solution)/shard_map/ppermute | solution.py:11
  783.5 10.3 %copy-start.1 = (bf16[1600,1536]{1,0:T(8,128)(2,1)}, bf16[1600,1536]{1,0:T(8,128)(2,1)S(1)}, u32[]{:S(2)}) copy-start(bf16[1600,1536]{1,0:T(8,128)(2,1)S(1)} %multiply_convert_fusion) | copy-start | bytes 14745604
  793.8 178.4 %all-to-all-start.1 = ((bf16[8,200,1024]{2,1,0:T(8,128)(2,1)}), bf16[8,200,1024]{2,1,0:T(8,128)(2,1)S(1)}, u32[]{:S(2)}, u32[]{:S(2)}) async-start(bf16[8,200,1024]{2,1,0:T(8,128)(2,1)} %bitcast.60), calls=%async_computation.1 | async-start | bytes 6553600 | tf_op jit(solution)/shard_map/all_to_all | solution.py:88
  921.9 28.7 %slice-start = ((s8[9437184]{0:T(1024)(128)(4,1)}), s8[4194304]{0:T(1024)(128)(4,1)S(1)}, s32[]{:S(2)}) async-start(s8[9437184]{0:T(1024)(128)(4,1)} %bitcast.50), calls=%async_computation.5 | async-start | bytes 8388608
  921.9 28.7 %slice-start.1 = ((s8[9437184]{0:T(1024)(128)(4,1)}), s8[4194304]{0:T(1024)(128)(4,1)S(1)}, s32[]{:S(2)}) async-start(s8[9437184]{0:T(1024)(128)(4,1)} %bitcast.50), calls=%async_computation.6 | async-start | bytes 8388608
  921.9 28.7 %slice-start.3 = ((s8[6291456]{0:T(1024)(128)(4,1)}), s8[4194304]{0:T(1024)(128)(4,1)S(1)}, s32[]{:S(2)}) async-start(s8[6291456]{0:T(1024)(128)(4,1)} %bitcast.52), calls=%async_computation.8 | async-start | bytes 8388608
  934.1 16.5 %slice-start.2 = ((s8[9437184]{0:T(1024)(128)(4,1)}), s8[1048576]{0:T(1024)(128)(4,1)S(1)}, s32[]{:S(2)}) async-start(s8[9437184]{0:T(1024)(128)(4,1)} %bitcast.50), calls=%async_computation.7 | async-start | bytes 2097152
  934.1 16.5 %slice-start.4 = ((s8[6291456]{0:T(1024)(128)(4,1)}), s8[2097152]{0:T(1024)(128)(4,1)S(1)}, s32[]{:S(2)}) async-start(s8[6291456]{0:T(1024)(128)(4,1)} %bitcast.52), calls=%async_computation.9 | async-start | bytes 4194304
  972.2 10.9 %copy-start.5 = (f32[320,4]{1,0:T(8,128)S(1)}, f32[320,4]{1,0:T(8,128)}, u32[]{:S(2)}) copy-start(f32[320,4]{1,0:T(8,128)} %copy-done.4) | copy-start | bytes 15364
Sparse Core Ops, SparseCore 0:
  86.2 656.5 all-gather.2
  745.1 176.6 all-reduce.3
